TPU v7x, 128 devices: a whole 4x4x4 slice. The times are simulated.
128 devices in a mesh: slab: 8 (over y, z_lo), row: 4 (over z_hi, core), col: 4 (over x).
Axes of the slice: x: 4, y: 4, z: 4 (z_hi: 2, z_lo: 2; z = z_hi * 2 + z_lo), core: 2. Of those that a mesh axis runs over, the one named last changes fastest.
Arguments:
- inverse: bfloat16 [8, 8192, 4, 2048], P('slab', 'row', None, 'col'), may hold values from -0.0625 to 0.0625
- sources: bfloat16 [8, 4, 8192, 128], P('slab', None, ('row', 'col')), may hold values from -6 to 6
- coupling: float32 [8, 2, 8192], P('slab', None, ('row', 'col')), may hold values from -1 to 1
- plan: int32 [6, 8, 2], replicated, may hold values from 0 to 3
Outputs:
- up_out: bfloat16 [8, 8192, 128], P('slab', ('row', 'col'))
- down_out: bfloat16 [8, 8192, 128], P('slab', ('row', 'col'))
Inputs may be any that keep to these rules, and one draw needn't show every extreme that they name: `plan`: each entry names one of the 4 stored batches of its slab.
All inputs are finite; a program needn't handle non-finite values.
Results may differ from a plain program's by a relative error of at most 0.023.
Values may be sent and summed in bfloat16 or wider, within the bound.
No kernel may reach another device: no remote copies, remote signals or barrier semaphores. Data moves between devices by JAX's collectives and lax.ppermute only.
A program may use at most 64 MiB of HBM per device.

v0:
```python
import jax
import jax.numpy as jnp
from jax import lax
from jax.sharding import PartitionSpec as P

TICKS = 6


def in_blocks(value, dim, count):
    lengths = value.shape
    pieces = value.reshape(*lengths[:dim], count, lengths[dim] // count, *lengths[dim + 1 :])
    return jnp.moveaxis(pieces, dim, 0)


def summed_on_arrival(value, axis, dim):
    count = lax.axis_size(axis)
    pieces = lax.all_to_all(in_blocks(value, dim, count), axis, 0, 0, tiled=True)
    return jnp.sum(pieces.astype(jnp.float32), axis=0)


def from_everyone(value, axis):
    count = lax.axis_size(axis)
    return lax.all_to_all(
        jnp.broadcast_to(value[None], (count, *value.shape)), axis, 0, 0, tiled=True
    )


def laid_out(pieces, dim):
    lengths = list(pieces.shape[1:])
    lengths[dim] *= pieces.shape[0]
    return jnp.moveaxis(pieces, 0, dim).reshape(lengths)


def collect(value, axis, dim):
    pieces = from_everyone(value, axis)
    return laid_out(pieces, dim)


def shifted(value, axis, steps):
    count = lax.axis_size(axis)
    leading, last = (max(0, -steps), min(count, count - steps))
    return lax.ppermute(value, axis, [(source, source + steps) for source in range(leading, last)])


def per_device(inverse, sources, coupling, plan):
    local_block = inverse[0]
    rows_here = local_block.shape[0]
    matrix = local_block.reshape(rows_here, -1)
    piece_rows = sources.shape[2]
    batch_width = sources.shape[3]
    slab_index = lax.axis_index("slab")
    up_gain = coupling[0, 0][:, None]
    down_gain = coupling[0, 1][:, None]
    stored = sources[0]
    up_out = jnp.zeros((piece_rows, batch_width), jnp.bfloat16)
    down_out = jnp.zeros((piece_rows, batch_width), jnp.bfloat16)
    for tick_index in range(TICKS):
        if tick_index == 0:
            up_recv = up_out
            down_recv = down_out
        else:
            up_recv = shifted(up_out, "slab", 1)
            down_recv = shifted(down_out, "slab", -1)
        up_choice = plan[tick_index, slab_index, 0]
        down_choice = plan[tick_index, slab_index, 1]
        up_source = lax.dynamic_index_in_dim(stored, up_choice, 0, keepdims=False)
        down_source = lax.dynamic_index_in_dim(stored, down_choice, 0, keepdims=False)
        up_in = (up_source.astype(jnp.float32) + up_gain * up_recv.astype(jnp.float32)).astype(
            jnp.bfloat16
        )
        down_in = (
            down_source.astype(jnp.float32) + down_gain * down_recv.astype(jnp.float32)
        ).astype(jnp.bfloat16)
        forward_partial_value = jnp.dot(
            matrix,
            lax.all_gather(up_in, "row", axis=0, tiled=True),
            preferred_element_type=jnp.float32,
        )
        forward_summed = summed_on_arrival(forward_partial_value.astype(jnp.bfloat16), "col", 0)
        up_out = forward_summed.astype(jnp.bfloat16)
        partial_value = lax.dot_general(
            matrix,
            collect(down_in, "col", 0),
            (((0,), (0,)), ((), ())),
            preferred_element_type=jnp.float32,
        )
        summed = summed_on_arrival(partial_value.astype(jnp.bfloat16), "row", 0)
        down_out = summed.astype(jnp.bfloat16)
    return (up_out[None], down_out[None])


def solution(mesh):
    placed = (
        P("slab", "row", None, "col"),
        P("slab", None, ("row", "col"), None),
        P("slab", None, ("row", "col")),
        P(),
    )
    return jax.shard_map(
        per_device,
        mesh=mesh,
        in_specs=placed,
        out_specs=(P("slab", ("row", "col"), None), P("slab", ("row", "col"), None)),
        check_vma=False,
    )
```

profile of v0, /device:TPU:16, one launch (start us, length us, event | category | flops | bytes accessed | tf_op | source)
XLA Modules:
  0.0 361.2 jit_solution(5221047215801752886)
XLA Ops:
  12.9 9.5 %all_gather.18 = bf16[2048,128]{1,0:T(8,128)(2,1)S(1)} all-gather(bf16[512,128]{1,0:T(8,128)(2,1)S(1)} %get-tuple-element.15), channel_id=1, replica_groups=mesh['slab'=8,'row'=4,'col'=4] {'row'}, dimensions={0}, use_global_device_ids=true | all-gather | bytes 655360 | tf_op jit(solution)/shard_map/all_gather | solution.py:76
  22.4 10.2 %copy.81 = bf16[256,8,4,512]{3,1,2,0:T(8,128)(2,1)} copy(bf16[256,8,4,512]{3,2,1,0:T(4,128)(2,1)} %bitcast.157) | data formatting | bytes 16777216
  32.6 6.3 %convolution_convert_fusion.11 = bf16[128,2048]{1,0:T(8,128)(2,1)S(1)} fusion(bf16[2048,128]{1,0:T(8,128)(2,1)S(1)} %all_gather.18, bf16[2048,2048]{1,0:T(8,128)(2,1)} %bitcast.145), kind=kOutput, calls=%fused_computation.11 | convolution fusion | flops 1074003968 | bytes 9437184 | tf_op jit(solution)/shard_map/dot_general | solution.py:74
  39.8 4.8 %all-to-all-start = ((bf16[4,512,128]{1,2,0:T(8,128)(2,1)}), bf16[4,512,128]{1,2,0:T(8,128)(2,1)S(1)}, u32[]{:S(2)}, u32[]{:S(2)}) async-start(bf16[4,512,128]{1,2,0:T(8,128)(2,1)} %bitcast.144), calls=%async_computation | async-start | bytes 1048576 | tf_op jit(solution)/shard_map/all_to_all | solution.py:17
  44.7 4.7 %convolution_convert_fusion.5 = bf16[128,2048]{1,0:T(8,128)(2,1)S(1)} fusion(bf16[2048,128]{1,0:T(8,128)(2,1)S(1)} %bitcast.158, bf16[2048,2048]{1,0:T(8,128)(2,1)} %bitcast.146), kind=kOutput, calls=%fused_computation.5 | convolution fusion | flops 1074003968 | bytes 9437184 | tf_op jit(solution)/shard_map/dot_general | solution.py:81
  80.1 5.4 %collective-permute-done = bf16[512,128]{0,1:T(8,128)(2,1)S(1)} collective-permute-done((bf16[512,128]{0,1:T(8,128)(2,1)S(1)}, bf16[512,128]{0,1:T(8,128)(2,1)S(1)}, u32[]{:S(2)}, u32[]{:S(2)}) %collective-permute-start) | collective-permute-done | bytes 131104 | tf_op jit(solution)/shard_map/ppermute | solution.py:42
  87.5 11.0 %all_gather.19 = bf16[2048,128]{0,1:T(8,128)(2,1)S(1)} all-gather(bf16[512,128]{0,1:T(8,128)(2,1)S(1)} %fusion.7), channel_id=1, replica_groups=mesh['slab'=8,'row'=4,'col'=4] {'row'}, dimensions={0}, use_global_device_ids=true | all-gather | bytes 655360 | tf_op jit(solution)/shard_map/all_gather | solution.py:76
  103.1 6.3 %convolution_convert_fusion.10 = bf16[128,2048]{1,0:T(8,128)(2,1)S(1)} fusion(bf16[2048,128]{0,1:T(8,128)(2,1)S(1)} %all_gather.19, bf16[2048,2048]{1,0:T(8,128)(2,1)} %bitcast.147), kind=kOutput, calls=%fused_computation.10 | convolution fusion | flops 1074003968 | bytes 9437184 | tf_op jit(solution)/shard_map/dot_general | solution.py:74
  117.0 4.7 %convolution_convert_fusion.4 = bf16[128,2048]{1,0:T(8,128)(2,1)S(1)} fusion(bf16[2048,128]{1,0:T(8,128)(2,1)S(1)} %bitcast.160, bf16[2048,2048]{1,0:T(8,128)(2,1)} %bitcast.148), kind=kOutput, calls=%fused_computation.4 | convolution fusion | flops 1074003968 | bytes 9437184 | tf_op jit(solution)/shard_map/dot_general | solution.py:81
  132.0 7.2 %collective-permute-done.1 = bf16[512,128]{0,1:T(8,128)(2,1)S(1)} collective-permute-done((bf16[512,128]{0,1:T(8,128)(2,1)S(1)}, bf16[512,128]{0,1:T(8,128)(2,1)S(1)}, u32[]{:S(2)}, u32[]{:S(2)}) %collective-permute-start.1) | collective-permute-done | bytes 131104 | tf_op jit(solution)/shard_map/ppermute | solution.py:42
  144.7 9.6 %all_gather.20 = bf16[2048,128]{0,1:T(8,128)(2,1)S(1)} all-gather(bf16[512,128]{0,1:T(8,128)(2,1)S(1)} %fusion.8), channel_id=1, replica_groups=mesh['slab'=8,'row'=4,'col'=4] {'row'}, dimensions={0}, use_global_device_ids=true | all-gather | bytes 655360 | tf_op jit(solution)/shard_map/all_gather | solution.py:76
  158.8 6.3 %convolution_convert_fusion.9 = bf16[128,2048]{1,0:T(8,128)(2,1)S(1)} fusion(bf16[2048,128]{0,1:T(8,128)(2,1)S(1)} %all_gather.20, bf16[2048,2048]{1,0:T(8,128)(2,1)} %bitcast.149), kind=kOutput, calls=%fused_computation.9 | convolution fusion | flops 1074003968 | bytes 9437184 | tf_op jit(solution)/shard_map/dot_general | solution.py:74
  172.6 4.7 %convolution_convert_fusion.3 = bf16[128,2048]{1,0:T(8,128)(2,1)S(1)} fusion(bf16[2048,128]{1,0:T(8,128)(2,1)S(1)} %bitcast.161, bf16[2048,2048]{1,0:T(8,128)(2,1)} %bitcast.150), kind=kOutput, calls=%fused_computation.3 | convolution fusion | flops 1074003968 | bytes 9437184 | tf_op jit(solution)/shard_map/dot_general | solution.py:81
  187.7 7.2 %collective-permute-done.2 = bf16[512,128]{0,1:T(8,128)(2,1)S(1)} collective-permute-done((bf16[512,128]{0,1:T(8,128)(2,1)S(1)}, bf16[512,128]{0,1:T(8,128)(2,1)S(1)}, u32[]{:S(2)}, u32[]{:S(2)}) %collective-permute-start.2) | collective-permute-done | bytes 131104 | tf_op jit(solution)/shard_map/ppermute | solution.py:42
  199.2 10.9 %all_gather.21 = bf16[2048,128]{0,1:T(8,128)(2,1)S(1)} all-gather(bf16[512,128]{0,1:T(8,128)(2,1)S(1)} %fusion.9), channel_id=1, replica_groups=mesh['slab'=8,'row'=4,'col'=4] {'row'}, dimensions={0}, use_global_device_ids=true | all-gather | bytes 655360 | tf_op jit(solution)/shard_map/all_gather | solution.py:76
  214.6 6.3 %convolution_convert_fusion.8 = bf16[128,2048]{1,0:T(8,128)(2,1)S(1)} fusion(bf16[2048,128]{0,1:T(8,128)(2,1)S(1)} %all_gather.21, bf16[2048,2048]{1,0:T(8,128)(2,1)} %bitcast.151), kind=kOutput, calls=%fused_computation.8 | convolution fusion | flops 1074003968 | bytes 9437184 | tf_op jit(solution)/shard_map/dot_general | solution.py:74
  228.3 4.7 %convolution_convert_fusion.2 = bf16[128,2048]{1,0:T(8,128)(2,1)S(1)} fusion(bf16[2048,128]{1,0:T(8,128)(2,1)S(1)} %bitcast.162, bf16[2048,2048]{1,0:T(8,128)(2,1)} %bitcast.152), kind=kOutput, calls=%fused_computation.2 | convolution fusion | flops 1074003968 | bytes 9437184 | tf_op jit(solution)/shard_map/dot_general | solution.py:81
  243.4 7.2 %collective-permute-done.3 = bf16[512,128]{0,1:T(8,128)(2,1)S(1)} collective-permute-done((bf16[512,128]{0,1:T(8,128)(2,1)S(1)}, bf16[512,128]{0,1:T(8,128)(2,1)S(1)}, u32[]{:S(2)}, u32[]{:S(2)}) %collective-permute-start.3) | collective-permute-done | bytes 131104 | tf_op jit(solution)/shard_map/ppermute | solution.py:42
  254.0 10.5 %all_gather.22 = bf16[2048,128]{0,1:T(8,128)(2,1)S(1)} all-gather(bf16[512,128]{0,1:T(8,128)(2,1)S(1)} %fusion.10), channel_id=1, replica_groups=mesh['slab'=8,'row'=4,'col'=4] {'row'}, dimensions={0}, use_global_device_ids=true | all-gather | bytes 655360 | tf_op jit(solution)/shard_map/all_gather | solution.py:76
  269.3 6.3 %convolution_convert_fusion.7 = bf16[128,2048]{1,0:T(8,128)(2,1)S(1)} fusion(bf16[2048,128]{0,1:T(8,128)(2,1)S(1)} %all_gather.22, bf16[2048,2048]{1,0:T(8,128)(2,1)} %bitcast.153), kind=kOutput, calls=%fused_computation.7 | convolution fusion | flops 1074003968 | bytes 9437184 | tf_op jit(solution)/shard_map/dot_general | solution.py:74
  298.0 7.2 %collective-permute-done.4 = bf16[512,128]{0,1:T(8,128)(2,1)S(1)} collective-permute-done((bf16[512,128]{0,1:T(8,128)(2,1)S(1)}, bf16[512,128]{0,1:T(8,128)(2,1)S(1)}, u32[]{:S(2)}, u32[]{:S(2)}) %collective-permute-start.4) | collective-permute-done | bytes 131104 | tf_op jit(solution)/shard_map/ppermute | solution.py:42
  308.5 10.5 %all_gather.23 = bf16[2048,128]{0,1:T(8,128)(2,1)S(1)} all-gather(bf16[512,128]{0,1:T(8,128)(2,1)S(1)} %fusion.11), channel_id=1, replica_groups=mesh['slab'=8,'row'=4,'col'=4] {'row'}, dimensions={0}, use_global_device_ids=true | all-gather | bytes 655360 | tf_op jit(solution)/shard_map/all_gather | solution.py:76
  323.6 6.3 %convolution_convert_fusion.6 = bf16[128,2048]{1,0:T(8,128)(2,1)S(1)} fusion(bf16[2048,128]{0,1:T(8,128)(2,1)S(1)} %all_gather.23, bf16[2048,2048]{1,0:T(8,128)(2,1)} %bitcast.155), kind=kOutput, calls=%fused_computation.6 | convolution fusion | flops 1074003968 | bytes 9437184 | tf_op jit(solution)/shard_map/dot_general | solution.py:74
  351.0 9.4 %all-to-all-done.17 = bf16[4,512,128]{1,2,0:T(8,128)(2,1)S(1)} async-done(((bf16[4,512,128]{1,2,0:T(8,128)(2,1)}), bf16[4,512,128]{1,2,0:T(8,128)(2,1)S(1)}, u32[]{:S(2)}, u32[]{:S(2)}) %all-to-all-start.17) | async-done | bytes 524320 | tf_op jit(solution)/shard_map/all_to_all | solution.py:17
  (115 shorter events, 161.1 us)
Async XLA Ops:
  8.6 31.3 %all-to-all-start.6 = ((bf16[4,512,128]{2,1,0:T(8,128)(2,1)}), bf16[4,512,128]{2,1,0:T(8,128)(2,1)S(1)}, u32[]{:S(2)}, u32[]{:S(2)}) async-start(bf16[4,512,128]{2,1,0:T(8,128)(2,1)} %broadcast_in_dim.17), calls=%async_computation.6 | async-start | bytes 1048576 | tf_op jit(solution)/shard_map/all_to_all | solution.py:23
  39.8 14.8 %all-to-all-start = ((bf16[4,512,128]{1,2,0:T(8,128)(2,1)}), bf16[4,512,128]{1,2,0:T(8,128)(2,1)S(1)}, u32[]{:S(2)}, u32[]{:S(2)}) async-start(bf16[4,512,128]{1,2,0:T(8,128)(2,1)} %bitcast.144), calls=%async_computation | async-start | bytes 1048576 | tf_op jit(solution)/shard_map/all_to_all | solution.py:17
  54.6 30.8 %all-to-all-start.7 = ((bf16[4,512,128]{1,2,0:T(8,128)(2,1)}), bf16[4,512,128]{1,2,0:T(8,128)(2,1)S(1)}, u32[]{:S(2)}, u32[]{:S(2)}) async-start(bf16[4,512,128]{1,2,0:T(8,128)(2,1)} %bitcast.138), calls=%async_computation.7 | async-start | bytes 1048576 | tf_op jit(solution)/shard_map/all_to_all | solution.py:17
  85.6 13.0 %collective-permute-start.5 = (bf16[512,128]{0,1:T(8,128)(2,1)S(1)}, bf16[512,128]{0,1:T(8,128)(2,1)S(1)}, u32[]{:S(2)}, u32[]{:S(2)}) collective-permute-start(bf16[512,128]{0,1:T(8,128)(2,1)S(1)} %reduce_sum.150), channel_id=1, source_target_pairs={{16,0},{32,16},{48,32},{64,48},{80,64},{96,80},{112,96},{17,1},{33... | collective-permute-start | bytes 393224 | tf_op jit(solution)/shard_map/ppermute | solution.py:42
  99.6 13.7 %all-to-all-start.8 = ((bf16[4,512,128]{2,1,0:T(8,128)(2,1)}), bf16[4,512,128]{2,1,0:T(8,128)(2,1)S(1)}, u32[]{:S(2)}, u32[]{:S(2)}) async-start(bf16[4,512,128]{2,1,0:T(8,128)(2,1)} %broadcast_in_dim.18), calls=%async_computation.8 | async-start | bytes 1048576 | tf_op jit(solution)/shard_map/all_to_all | solution.py:23
  113.3 12.9 %all-to-all-start.1 = ((bf16[4,512,128]{1,2,0:T(8,128)(2,1)}), bf16[4,512,128]{1,2,0:T(8,128)(2,1)S(1)}, u32[]{:S(2)}, u32[]{:S(2)}) async-start(bf16[4,512,128]{1,2,0:T(8,128)(2,1)} %bitcast.143), calls=%async_computation.1 | async-start | bytes 1048576 | tf_op jit(solution)/shard_map/all_to_all | solution.py:17
  126.2 14.3 %all-to-all-start.9 = ((bf16[4,512,128]{1,2,0:T(8,128)(2,1)}), bf16[4,512,128]{1,2,0:T(8,128)(2,1)S(1)}, u32[]{:S(2)}, u32[]{:S(2)}) async-start(bf16[4,512,128]{1,2,0:T(8,128)(2,1)} %bitcast.137), calls=%async_computation.9 | async-start | bytes 1048576 | tf_op jit(solution)/shard_map/all_to_all | solution.py:17
  129.7 9.4 %collective-permute-start.1 = (bf16[512,128]{0,1:T(8,128)(2,1)S(1)}, bf16[512,128]{0,1:T(8,128)(2,1)S(1)}, u32[]{:S(2)}, u32[]{:S(2)}) collective-permute-start(bf16[512,128]{0,1:T(8,128)(2,1)S(1)} %reduce_sum.145), channel_id=1, source_target_pairs={{0,16},{16,32},{32,48},{48,64},{64,80},{80,96},{96,112},{1,17},{17... | collective-permute-start | bytes 393224 | tf_op jit(solution)/shard_map/ppermute | solution.py:42
  140.6 13.7 %collective-permute-start.6 = (bf16[512,128]{0,1:T(8,128)(2,1)S(1)}, bf16[512,128]{0,1:T(8,128)(2,1)S(1)}, u32[]{:S(2)}, u32[]{:S(2)}) collective-permute-start(bf16[512,128]{0,1:T(8,128)(2,1)S(1)} %reduce_sum.151), channel_id=1, source_target_pairs={{16,0},{32,16},{48,32},{64,48},{80,64},{96,80},{112,96},{17,1},{33... | collective-permute-start | bytes 393224 | tf_op jit(solution)/shard_map/ppermute | solution.py:42
  155.4 13.7 %all-to-all-start.10 = ((bf16[4,512,128]{2,1,0:T(8,128)(2,1)}), bf16[4,512,128]{2,1,0:T(8,128)(2,1)S(1)}, u32[]{:S(2)}, u32[]{:S(2)}) async-start(bf16[4,512,128]{2,1,0:T(8,128)(2,1)} %broadcast_in_dim.19), calls=%async_computation.10 | async-start | bytes 1048576 | tf_op jit(solution)/shard_map/all_to_all | solution.py:23
  169.1 12.9 %all-to-all-start.2 = ((bf16[4,512,128]{1,2,0:T(8,128)(2,1)}), bf16[4,512,128]{1,2,0:T(8,128)(2,1)S(1)}, u32[]{:S(2)}, u32[]{:S(2)}) async-start(bf16[4,512,128]{1,2,0:T(8,128)(2,1)} %bitcast.142), calls=%async_computation.2 | async-start | bytes 1048576 | tf_op jit(solution)/shard_map/all_to_all | solution.py:17
  181.9 14.3 %all-to-all-start.11 = ((bf16[4,512,128]{1,2,0:T(8,128)(2,1)}), bf16[4,512,128]{1,2,0:T(8,128)(2,1)S(1)}, u32[]{:S(2)}, u32[]{:S(2)}) async-start(bf16[4,512,128]{1,2,0:T(8,128)(2,1)} %bitcast.136), calls=%async_computation.11 | async-start | bytes 1048576 | tf_op jit(solution)/shard_map/all_to_all | solution.py:17
  196.4 13.7 %collective-permute-start.7 = (bf16[512,128]{0,1:T(8,128)(2,1)S(1)}, bf16[512,128]{0,1:T(8,128)(2,1)S(1)}, u32[]{:S(2)}, u32[]{:S(2)}) collective-permute-start(bf16[512,128]{0,1:T(8,128)(2,1)S(1)} %reduce_sum.152), channel_id=1, source_target_pairs={{16,0},{32,16},{48,32},{64,48},{80,64},{96,80},{112,96},{17,1},{33... | collective-permute-start | bytes 393224 | tf_op jit(solution)/shard_map/ppermute | solution.py:42
  211.1 13.7 %all-to-all-start.12 = ((bf16[4,512,128]{2,1,0:T(8,128)(2,1)}), bf16[4,512,128]{2,1,0:T(8,128)(2,1)S(1)}, u32[]{:S(2)}, u32[]{:S(2)}) async-start(bf16[4,512,128]{2,1,0:T(8,128)(2,1)} %broadcast_in_dim.20), calls=%async_computation.12 | async-start | bytes 1048576 | tf_op jit(solution)/shard_map/all_to_all | solution.py:23
  224.8 12.9 %all-to-all-start.3 = ((bf16[4,512,128]{1,2,0:T(8,128)(2,1)}), bf16[4,512,128]{1,2,0:T(8,128)(2,1)S(1)}, u32[]{:S(2)}, u32[]{:S(2)}) async-start(bf16[4,512,128]{1,2,0:T(8,128)(2,1)} %bitcast.141), calls=%async_computation.3 | async-start | bytes 1048576 | tf_op jit(solution)/shard_map/all_to_all | solution.py:17
  237.7 14.3 %all-to-all-start.13 = ((bf16[4,512,128]{1,2,0:T(8,128)(2,1)}), bf16[4,512,128]{1,2,0:T(8,128)(2,1)S(1)}, u32[]{:S(2)}, u32[]{:S(2)}) async-start(bf16[4,512,128]{1,2,0:T(8,128)(2,1)} %bitcast.135), calls=%async_computation.13 | async-start | bytes 1048576 | tf_op jit(solution)/shard_map/all_to_all | solution.py:17
  252.1 12.4 %collective-permute-start.8 = (bf16[512,128]{0,1:T(8,128)(2,1)S(1)}, bf16[512,128]{0,1:T(8,128)(2,1)S(1)}, u32[]{:S(2)}, u32[]{:S(2)}) collective-permute-start(bf16[512,128]{0,1:T(8,128)(2,1)S(1)} %reduce_sum.153), channel_id=1, source_target_pairs={{16,0},{32,16},{48,32},{64,48},{80,64},{96,80},{112,96},{17,1},{33... | collective-permute-start | bytes 393224 | tf_op jit(solution)/shard_map/ppermute | solution.py:42
  265.6 13.7 %all-to-all-start.14 = ((bf16[4,512,128]{2,1,0:T(8,128)(2,1)}), bf16[4,512,128]{2,1,0:T(8,128)(2,1)S(1)}, u32[]{:S(2)}, u32[]{:S(2)}) async-start(bf16[4,512,128]{2,1,0:T(8,128)(2,1)} %broadcast_in_dim.21), calls=%async_computation.14 | async-start | bytes 1048576 | tf_op jit(solution)/shard_map/all_to_all | solution.py:23
  279.3 12.9 %all-to-all-start.4 = ((bf16[4,512,128]{1,2,0:T(8,128)(2,1)}), bf16[4,512,128]{1,2,0:T(8,128)(2,1)S(1)}, u32[]{:S(2)}, u32[]{:S(2)}) async-start(bf16[4,512,128]{1,2,0:T(8,128)(2,1)} %bitcast.140), calls=%async_computation.4 | async-start | bytes 1048576 | tf_op jit(solution)/shard_map/all_to_all | solution.py:17
  292.2 14.3 %all-to-all-start.15 = ((bf16[4,512,128]{1,2,0:T(8,128)(2,1)}), bf16[4,512,128]{1,2,0:T(8,128)(2,1)S(1)}, u32[]{:S(2)}, u32[]{:S(2)}) async-start(bf16[4,512,128]{1,2,0:T(8,128)(2,1)} %bitcast.134), calls=%async_computation.15 | async-start | bytes 1048576 | tf_op jit(solution)/shard_map/all_to_all | solution.py:17
  306.6 12.4 %collective-permute-start.9 = (bf16[512,128]{0,1:T(8,128)(2,1)S(1)}, bf16[512,128]{0,1:T(8,128)(2,1)S(1)}, u32[]{:S(2)}, u32[]{:S(2)}) collective-permute-start(bf16[512,128]{0,1:T(8,128)(2,1)S(1)} %reduce_sum.154), channel_id=1, source_target_pairs={{16,0},{32,16},{48,32},{64,48},{80,64},{96,80},{112,96},{17,1},{33... | collective-permute-start | bytes 393224 | tf_op jit(solution)/shard_map/ppermute | solution.py:42
  320.1 13.7 %all-to-all-start.16 = ((bf16[4,512,128]{2,1,0:T(8,128)(2,1)}), bf16[4,512,128]{2,1,0:T(8,128)(2,1)S(1)}, u32[]{:S(2)}, u32[]{:S(2)}) async-start(bf16[4,512,128]{2,1,0:T(8,128)(2,1)} %broadcast_in_dim.22), calls=%async_computation.16 | async-start | bytes 1048576 | tf_op jit(solution)/shard_map/all_to_all | solution.py:23
  333.8 12.9 %all-to-all-start.5 = ((bf16[4,512,128]{1,2,0:T(8,128)(2,1)}), bf16[4,512,128]{1,2,0:T(8,128)(2,1)S(1)}, u32[]{:S(2)}, u32[]{:S(2)}) async-start(bf16[4,512,128]{1,2,0:T(8,128)(2,1)} %bitcast.139), calls=%async_computation.5 | async-start | bytes 1048576 | tf_op jit(solution)/shard_map/all_to_all | solution.py:17
  346.6 13.8 %all-to-all-start.17 = ((bf16[4,512,128]{1,2,0:T(8,128)(2,1)}), bf16[4,512,128]{1,2,0:T(8,128)(2,1)S(1)}, u32[]{:S(2)}, u32[]{:S(2)}) async-start(bf16[4,512,128]{1,2,0:T(8,128)(2,1)} %bitcast.133), calls=%async_computation.17 | async-start | bytes 1048576 | tf_op jit(solution)/shard_map/all_to_all | solution.py:17
  (5 other events, 72.0 us)
where the time goes:
time: 363 us; the launch traced here: 361 us
  starting transfers between devices  88.6 us (24%)
  waiting for transfers between devices  87.6 us (24%)
  matrix products  65.7 us (18%)
  blocking collectives  62 us (17%)
  local copies, waits for them, and re-layouts  31.7 us (9%)
  between operations  23.1 us (6%)
    all_gather x6, blocking collectives, per_device(): lax.all_gather(up_in, 'row', axis=0, tiled=True)  62 us
    all_to_all x12, starting transfers between devices, summed_on_arrival(): lax.all_to_all(in_blocks(value, dim, count), axis, 0, 0, tiled=True)  43.3 us
    all_to_all x12, waiting for transfers between devices, summed_on_arrival(): lax.all_to_all(in_blocks(value, dim, count), axis, 0, 0, tiled=True)  38.1 us
    dot_general x6, matrix products, per_device(): jnp.dot(matrix, lax.all_gather(up_in, 'row', axis=0, tiled=True), preferr...  37.6 us
    ppermute x10, waiting for transfers between devices, shifted(): lax.ppermute(value, axis, [(source, source + steps) for source in range(l...  34.2 us
    dot_general x6, matrix products, per_device(): lax.dot_general(matrix, collect(down_in, 'col', 0), (((0,), (0,)), ((), (...  28 us
    ppermute x10, starting transfers between devices, shifted(): lax.ppermute(value, axis, [(source, source + steps) for source in range(l...  23.5 us
    all_to_all x6, starting transfers between devices, from_everyone(): lax.all_to_all(jnp.broadcast_to(value[None], (count, *value.shape)), axis...  21.9 us
  transfers between devices with their start and end apart: 28, of which 21 were waited for; matrix products, arithmetic and copies ran while one was open for 25% of the time, Pallas kernels for 0%

commit v1 on v0

--- a/solution.py
+++ b/solution.py
@@ -71,10 +71,15 @@
         down_in = (
             down_source.astype(jnp.float32) + down_gain * down_recv.astype(jnp.float32)
         ).astype(jnp.bfloat16)
+
+        def _open_blocks(xin):
+            finding = lax.axis_size("row")
+            everything = jnp.stack([xin] * finding, axis=0)
+            newest = lax.all_to_all(everything, "row", split_axis=0, concat_axis=0)
+            return jnp.concatenate(newest, axis=0)
+
         forward_partial_value = jnp.dot(
-            matrix,
-            lax.all_gather(up_in, "row", axis=0, tiled=True),
-            preferred_element_type=jnp.float32,
+            matrix, _open_blocks(up_in), preferred_element_type=jnp.float32
         )
         forward_summed = summed_on_arrival(forward_partial_value.astype(jnp.bfloat16), "col", 0)
         up_out = forward_summed.astype(jnp.bfloat16)

time: 363 us -> 376 us (1.036)
  blocking collectives: 62 us -> 0 us
  waiting for transfers between devices: 87.6 us -> 128 us
  starting transfers between devices: 88.6 us -> 115 us
  local copies, waits for them, and re-layouts: 31.7 us -> 37.9 us
    all_gather x6 -> x0, blocking collectives: 62 us -> none  [per_device(): lax.all_gather(up_in, 'row', axis=0, tiled=True)]
    ppermute x10, waiting for transfers between devices: 34.2 us -> 75 us  [shifted(): lax.ppermute(value, axis, [(source, source + steps) for source in range(l...]
    all_to_all x0 -> x6, starting transfers between devices: none -> 23.4 us  [_open_blocks(): newest = lax.all_to_all(everything, 'row', split_axis=0, concat_axis=0)]
    all_to_all x0 -> x6, waiting for transfers between devices: none -> 8.07 us  [_open_blocks(): newest = lax.all_to_all(everything, 'row', split_axis=0, concat_axis=0)]
    all_to_all x12, waiting for transfers between devices: 38.1 us -> 31.5 us  [summed_on_arrival(): lax.all_to_all(in_blocks(value, dim, count), axis, 0, 0, tiled=True)]
    another operation x0 -> x6, local copies, waits for them, and re-layouts: none -> 5.61 us  [_open_blocks(): everything = jnp.stack([xin] * finding, axis=0)]
  transfers between devices with their start and end apart: 28 -> 34, of which waited for: 21 -> 32; matrix products, arithmetic and copies ran while one was open for 25% -> 24% of each run, Pallas kernels for 0% -> 0%
where the time goes in v1:
time: 376 us; the launch traced here: 374 us
  waiting for transfers between devices  128 us (34%)
  starting transfers between devices  115 us (31%)
  matrix products  65.8 us (18%)
  local copies, waits for them, and re-layouts  37.9 us (10%)
  between operations  24 us (6%)
    ppermute x10, waiting for transfers between devices, shifted(): lax.ppermute(value, axis, [(source, source + steps) for source in range(l...  75 us
    all_to_all x12, starting transfers between devices, summed_on_arrival(): lax.all_to_all(in_blocks(value, dim, count), axis, 0, 0, tiled=True)  43.4 us
    dot_general x6, matrix products, per_device(): jnp.dot(matrix, _open_blocks(up_in), preferred_element_type=jnp.float32)  37.8 us
    all_to_all x12, waiting for transfers between devices, summed_on_arrival(): lax.all_to_all(in_blocks(value, dim, count), axis, 0, 0, tiled=True)  31.5 us
    dot_general x6, matrix products, per_device(): lax.dot_general(matrix, collect(down_in, 'col', 0), (((0,), (0,)), ((), (...  28 us
    ppermute x10, starting transfers between devices, shifted(): lax.ppermute(value, axis, [(source, source + steps) for source in range(l...  26.3 us
    all_to_all x6, starting transfers between devices, _open_blocks(): newest = lax.all_to_all(everything, 'row', split_axis=0, concat_axis=0)  23.4 us
    all_to_all x6, starting transfers between devices, from_everyone(): lax.all_to_all(jnp.broadcast_to(value[None], (count, *value.shape)), axis...  21.9 us
  transfers between devices with their start and end apart: 34, of which 32 were waited for; matrix products, arithmetic and copies ran while one was open for 24% of the time, Pallas kernels for 0%

profile of v1, /device:TPU:16, one launch (start us, length us, event | category | flops | bytes accessed | tf_op | source)
XLA Modules:
  0.0 373.5 jit_solution(11757599754837230832)
XLA Ops:
  9.0 5.1 %all-to-all-start = ((bf16[4,512,128]{2,1,0:T(8,128)(2,1)}), bf16[4,512,128]{2,1,0:T(8,128)(2,1)S(1)}, u32[]{:S(2)}, u32[]{:S(2)}) async-start(bf16[4,512,128]{2,1,0:T(8,128)(2,1)} %stack.12), calls=%async_computation | async-start | bytes 1048576 | tf_op jit(solution)/shard_map/all_to_all | solution.py:78
  14.2 10.3 %copy.86 = bf16[256,8,4,512]{3,1,2,0:T(8,128)(2,1)} copy(bf16[256,8,4,512]{3,2,1,0:T(4,128)(2,1)} %bitcast.163) | data formatting | bytes 16777216
  29.7 6.3 %convolution_convert_fusion.11 = bf16[128,2048]{1,0:T(8,128)(2,1)S(1)} fusion(bf16[2048,128]{1,0:T(8,128)(2,1)S(1)} %bitcast.175, bf16[2048,2048]{1,0:T(8,128)(2,1)} %bitcast.151), kind=kOutput, calls=%fused_computation.11 | convolution fusion | flops 1074003968 | bytes 9437184 | tf_op jit(solution)/shard_map/dot_general | solution.py:81
  43.3 4.7 %convolution_convert_fusion.5 = bf16[128,2048]{1,0:T(8,128)(2,1)S(1)} fusion(bf16[2048,128]{1,0:T(8,128)(2,1)S(1)} %bitcast.165, bf16[2048,2048]{1,0:T(8,128)(2,1)} %bitcast.152), kind=kOutput, calls=%fused_computation.5 | convolution fusion | flops 1074003968 | bytes 9437184 | tf_op jit(solution)/shard_map/dot_general | solution.py:86
  78.7 5.5 %collective-permute-done = bf16[512,128]{0,1:T(8,128)(2,1)S(1)} collective-permute-done((bf16[512,128]{0,1:T(8,128)(2,1)S(1)}, bf16[512,128]{0,1:T(8,128)(2,1)S(1)}, u32[]{:S(2)}, u32[]{:S(2)}) %collective-permute-start) | collective-permute-done | bytes 131104 | tf_op jit(solution)/shard_map/ppermute | solution.py:42
  91.9 8.0 %collective-permute-done.5 = bf16[512,128]{0,1:T(8,128)(2,1)S(1)} collective-permute-done((bf16[512,128]{0,1:T(8,128)(2,1)S(1)}, bf16[512,128]{0,1:T(8,128)(2,1)S(1)}, u32[]{:S(2)}, u32[]{:S(2)}) %collective-permute-start.5) | collective-permute-done | bytes 131104 | tf_op jit(solution)/shard_map/ppermute | solution.py:42
  107.2 6.3 %convolution_convert_fusion.10 = bf16[128,2048]{1,0:T(8,128)(2,1)S(1)} fusion(bf16[2048,128]{1,0:T(8,128)(2,1)S(1)} %bitcast.171, bf16[2048,2048]{1,0:T(8,128)(2,1)} %bitcast.153), kind=kOutput, calls=%fused_computation.10 | convolution fusion | flops 1074003968 | bytes 9437184 | tf_op jit(solution)/shard_map/dot_general | solution.py:81
  134.0 7.4 %collective-permute-done.1 = bf16[512,128]{0,1:T(8,128)(2,1)S(1)} collective-permute-done((bf16[512,128]{0,1:T(8,128)(2,1)S(1)}, bf16[512,128]{0,1:T(8,128)(2,1)S(1)}, u32[]{:S(2)}, u32[]{:S(2)}) %collective-permute-start.1) | collective-permute-done | bytes 131104 | tf_op jit(solution)/shard_map/ppermute | solution.py:42
  150.8 8.0 %collective-permute-done.6 = bf16[512,128]{0,1:T(8,128)(2,1)S(1)} collective-permute-done((bf16[512,128]{0,1:T(8,128)(2,1)S(1)}, bf16[512,128]{0,1:T(8,128)(2,1)S(1)}, u32[]{:S(2)}, u32[]{:S(2)}) %collective-permute-start.6) | collective-permute-done | bytes 131104 | tf_op jit(solution)/shard_map/ppermute | solution.py:42
  164.6 6.3 %convolution_convert_fusion.9 = bf16[128,2048]{1,0:T(8,128)(2,1)S(1)} fusion(bf16[2048,128]{1,0:T(8,128)(2,1)S(1)} %bitcast.172, bf16[2048,2048]{1,0:T(8,128)(2,1)} %bitcast.155), kind=kOutput, calls=%fused_computation.9 | convolution fusion | flops 1074003968 | bytes 9437184 | tf_op jit(solution)/shard_map/dot_general | solution.py:81
  177.5 4.7 %convolution_convert_fusion.3 = bf16[128,2048]{1,0:T(8,128)(2,1)S(1)} fusion(bf16[2048,128]{1,0:T(8,128)(2,1)S(1)} %bitcast.167, bf16[2048,2048]{1,0:T(8,128)(2,1)} %bitcast.156), kind=kOutput, calls=%fused_computation.3 | convolution fusion | flops 1074003968 | bytes 9437184 | tf_op jit(solution)/shard_map/dot_general | solution.py:86
  191.6 7.4 %collective-permute-done.2 = bf16[512,128]{0,1:T(8,128)(2,1)S(1)} collective-permute-done((bf16[512,128]{0,1:T(8,128)(2,1)S(1)}, bf16[512,128]{0,1:T(8,128)(2,1)S(1)}, u32[]{:S(2)}, u32[]{:S(2)}) %collective-permute-start.2) | collective-permute-done | bytes 131104 | tf_op jit(solution)/shard_map/ppermute | solution.py:42
  208.4 8.0 %collective-permute-done.7 = bf16[512,128]{0,1:T(8,128)(2,1)S(1)} collective-permute-done((bf16[512,128]{0,1:T(8,128)(2,1)S(1)}, bf16[512,128]{0,1:T(8,128)(2,1)S(1)}, u32[]{:S(2)}, u32[]{:S(2)}) %collective-permute-start.7) | collective-permute-done | bytes 131104 | tf_op jit(solution)/shard_map/ppermute | solution.py:42
  222.2 6.3 %convolution_convert_fusion.8 = bf16[128,2048]{1,0:T(8,128)(2,1)S(1)} fusion(bf16[2048,128]{1,0:T(8,128)(2,1)S(1)} %bitcast.173, bf16[2048,2048]{1,0:T(8,128)(2,1)} %bitcast.157), kind=kOutput, calls=%fused_computation.8 | convolution fusion | flops 1074003968 | bytes 9437184 | tf_op jit(solution)/shard_map/dot_general | solution.py:81
  235.1 4.7 %convolution_convert_fusion.2 = bf16[128,2048]{1,0:T(8,128)(2,1)S(1)} fusion(bf16[2048,128]{1,0:T(8,128)(2,1)S(1)} %bitcast.168, bf16[2048,2048]{1,0:T(8,128)(2,1)} %bitcast.158), kind=kOutput, calls=%fused_computation.2 | convolution fusion | flops 1074003968 | bytes 9437184 | tf_op jit(solution)/shard_map/dot_general | solution.py:86
  249.2 7.4 %collective-permute-done.3 = bf16[512,128]{0,1:T(8,128)(2,1)S(1)} collective-permute-done((bf16[512,128]{0,1:T(8,128)(2,1)S(1)}, bf16[512,128]{0,1:T(8,128)(2,1)S(1)}, u32[]{:S(2)}, u32[]{:S(2)}) %collective-permute-start.3) | collective-permute-done | bytes 131104 | tf_op jit(solution)/shard_map/ppermute | solution.py:42
  266.0 8.0 %collective-permute-done.8 = bf16[512,128]{0,1:T(8,128)(2,1)S(1)} collective-permute-done((bf16[512,128]{0,1:T(8,128)(2,1)S(1)}, bf16[512,128]{0,1:T(8,128)(2,1)S(1)}, u32[]{:S(2)}, u32[]{:S(2)}) %collective-permute-start.8) | collective-permute-done | bytes 131104 | tf_op jit(solution)/shard_map/ppermute | solution.py:42
  280.0 6.3 %convolution_convert_fusion.7 = bf16[128,2048]{1,0:T(8,128)(2,1)S(1)} fusion(bf16[2048,128]{1,0:T(8,128)(2,1)S(1)} %bitcast.174, bf16[2048,2048]{1,0:T(8,128)(2,1)} %bitcast.159), kind=kOutput, calls=%fused_computation.7 | convolution fusion | flops 1074003968 | bytes 9437184 | tf_op jit(solution)/shard_map/dot_general | solution.py:81
  292.7 4.7 %convolution_convert_fusion.1 = bf16[128,2048]{1,0:T(8,128)(2,1)S(1)} fusion(bf16[2048,128]{1,0:T(8,128)(2,1)S(1)} %bitcast.169, bf16[2048,2048]{1,0:T(8,128)(2,1)} %bitcast.160), kind=kOutput, calls=%fused_computation.1 | convolution fusion | flops 1074003968 | bytes 9437184 | tf_op jit(solution)/shard_map/dot_general | solution.py:86
  306.9 7.4 %collective-permute-done.4 = bf16[512,128]{0,1:T(8,128)(2,1)S(1)} collective-permute-done((bf16[512,128]{0,1:T(8,128)(2,1)S(1)}, bf16[512,128]{0,1:T(8,128)(2,1)S(1)}, u32[]{:S(2)}, u32[]{:S(2)}) %collective-permute-start.4) | collective-permute-done | bytes 131104 | tf_op jit(solution)/shard_map/ppermute | solution.py:42
  323.7 8.0 %collective-permute-done.9 = bf16[512,128]{0,1:T(8,128)(2,1)S(1)} collective-permute-done((bf16[512,128]{0,1:T(8,128)(2,1)S(1)}, bf16[512,128]{0,1:T(8,128)(2,1)S(1)}, u32[]{:S(2)}, u32[]{:S(2)}) %collective-permute-start.9) | collective-permute-done | bytes 131104 | tf_op jit(solution)/shard_map/ppermute | solution.py:42
  337.5 6.3 %convolution_convert_fusion.6 = bf16[128,2048]{1,0:T(8,128)(2,1)S(1)} fusion(bf16[2048,128]{1,0:T(8,128)(2,1)S(1)} %bitcast.170, bf16[2048,2048]{1,0:T(8,128)(2,1)} %bitcast.161), kind=kOutput, calls=%fused_computation.6 | convolution fusion | flops 1074003968 | bytes 9437184 | tf_op jit(solution)/shard_map/dot_general | solution.py:81
  350.4 4.7 %convolution_convert_fusion = bf16[128,2048]{1,0:T(8,128)(2,1)S(1)} fusion(bf16[2048,128]{1,0:T(8,128)(2,1)S(1)} %bitcast.164, bf16[2048,2048]{1,0:T(8,128)(2,1)} %bitcast.162), kind=kOutput, calls=%fused_computation | convolution fusion | flops 1074003968 | bytes 9437184 | tf_op jit(solution)/shard_map/dot_general | solution.py:86
  363.2 9.5 %all-to-all-done.23 = bf16[4,512,128]{1,2,0:T(8,128)(2,1)S(1)} async-done(((bf16[4,512,128]{1,2,0:T(8,128)(2,1)}), bf16[4,512,128]{1,2,0:T(8,128)(2,1)S(1)}, u32[]{:S(2)}, u32[]{:S(2)}) %all-to-all-start.23) | async-done | bytes 524320 | tf_op jit(solution)/shard_map/all_to_all | solution.py:17
  (132 shorter events, 188.5 us)
Async XLA Ops:
  9.0 15.5 %all-to-all-start = ((bf16[4,512,128]{2,1,0:T(8,128)(2,1)}), bf16[4,512,128]{2,1,0:T(8,128)(2,1)S(1)}, u32[]{:S(2)}, u32[]{:S(2)}) async-start(bf16[4,512,128]{2,1,0:T(8,128)(2,1)} %stack.12), calls=%async_computation | async-start | bytes 1048576 | tf_op jit(solution)/shard_map/all_to_all | solution.py:78
  25.4 14.4 %all-to-all-start.12 = ((bf16[4,512,128]{2,1,0:T(8,128)(2,1)}), bf16[4,512,128]{2,1,0:T(8,128)(2,1)S(1)}, u32[]{:S(2)}, u32[]{:S(2)}) async-start(bf16[4,512,128]{2,1,0:T(8,128)(2,1)} %broadcast_in_dim.17), calls=%async_computation.12 | async-start | bytes 1048576 | tf_op jit(solution)/shard_map/all_to_all | solution.py:23
  39.8 12.7 %all-to-all-start.1 = ((bf16[4,512,128]{1,2,0:T(8,128)(2,1)}), bf16[4,512,128]{1,2,0:T(8,128)(2,1)S(1)}, u32[]{:S(2)}, u32[]{:S(2)}) async-start(bf16[4,512,128]{1,2,0:T(8,128)(2,1)} %bitcast.150), calls=%async_computation.1 | async-start | bytes 1048576 | tf_op jit(solution)/shard_map/all_to_all | solution.py:17
  52.5 31.8 %all-to-all-start.13 = ((bf16[4,512,128]{1,2,0:T(8,128)(2,1)}), bf16[4,512,128]{1,2,0:T(8,128)(2,1)S(1)}, u32[]{:S(2)}, u32[]{:S(2)}) async-start(bf16[4,512,128]{1,2,0:T(8,128)(2,1)} %bitcast.144), calls=%async_computation.13 | async-start | bytes 1048576 | tf_op jit(solution)/shard_map/all_to_all | solution.py:17
  85.3 17.5 %all-to-all-start.2 = ((bf16[4,512,128]{2,1,0:T(8,128)(2,1)}), bf16[4,512,128]{2,1,0:T(8,128)(2,1)S(1)}, u32[]{:S(2)}, u32[]{:S(2)}) async-start(bf16[4,512,128]{2,1,0:T(8,128)(2,1)} %stack.13), calls=%async_computation.2 | async-start | bytes 1048576 | tf_op jit(solution)/shard_map/all_to_all | solution.py:78
  103.7 12.9 %all-to-all-start.14 = ((bf16[4,512,128]{2,1,0:T(8,128)(2,1)}), bf16[4,512,128]{2,1,0:T(8,128)(2,1)S(1)}, u32[]{:S(2)}, u32[]{:S(2)}) async-start(bf16[4,512,128]{2,1,0:T(8,128)(2,1)} %broadcast_in_dim.18), calls=%async_computation.14 | async-start | bytes 1048576 | tf_op jit(solution)/shard_map/all_to_all | solution.py:23
  116.6 11.8 %all-to-all-start.3 = ((bf16[4,512,128]{1,2,0:T(8,128)(2,1)}), bf16[4,512,128]{1,2,0:T(8,128)(2,1)S(1)}, u32[]{:S(2)}, u32[]{:S(2)}) async-start(bf16[4,512,128]{1,2,0:T(8,128)(2,1)} %bitcast.149), calls=%async_computation.3 | async-start | bytes 1048576 | tf_op jit(solution)/shard_map/all_to_all | solution.py:17
  128.4 14.3 %all-to-all-start.15 = ((bf16[4,512,128]{1,2,0:T(8,128)(2,1)}), bf16[4,512,128]{1,2,0:T(8,128)(2,1)S(1)}, u32[]{:S(2)}, u32[]{:S(2)}) async-start(bf16[4,512,128]{1,2,0:T(8,128)(2,1)} %bitcast.143), calls=%async_computation.15 | async-start | bytes 1048576 | tf_op jit(solution)/shard_map/all_to_all | solution.py:17
  143.6 16.6 %all-to-all-start.4 = ((bf16[4,512,128]{2,1,0:T(8,128)(2,1)}), bf16[4,512,128]{2,1,0:T(8,128)(2,1)S(1)}, u32[]{:S(2)}, u32[]{:S(2)}) async-start(bf16[4,512,128]{2,1,0:T(8,128)(2,1)} %stack.14), calls=%async_computation.4 | async-start | bytes 1048576 | tf_op jit(solution)/shard_map/all_to_all | solution.py:78
  161.1 12.9 %all-to-all-start.16 = ((bf16[4,512,128]{2,1,0:T(8,128)(2,1)}), bf16[4,512,128]{2,1,0:T(8,128)(2,1)S(1)}, u32[]{:S(2)}, u32[]{:S(2)}) async-start(bf16[4,512,128]{2,1,0:T(8,128)(2,1)} %broadcast_in_dim.19), calls=%async_computation.16 | async-start | bytes 1048576 | tf_op jit(solution)/shard_map/all_to_all | solution.py:23
  174.0 11.8 %all-to-all-start.5 = ((bf16[4,512,128]{1,2,0:T(8,128)(2,1)}), bf16[4,512,128]{1,2,0:T(8,128)(2,1)S(1)}, u32[]{:S(2)}, u32[]{:S(2)}) async-start(bf16[4,512,128]{1,2,0:T(8,128)(2,1)} %bitcast.148), calls=%async_computation.5 | async-start | bytes 1048576 | tf_op jit(solution)/shard_map/all_to_all | solution.py:17
  185.7 14.6 %all-to-all-start.17 = ((bf16[4,512,128]{1,2,0:T(8,128)(2,1)}), bf16[4,512,128]{1,2,0:T(8,128)(2,1)S(1)}, u32[]{:S(2)}, u32[]{:S(2)}) async-start(bf16[4,512,128]{1,2,0:T(8,128)(2,1)} %bitcast.142), calls=%async_computation.17 | async-start | bytes 1048576 | tf_op jit(solution)/shard_map/all_to_all | solution.py:17
  201.3 16.6 %all-to-all-start.6 = ((bf16[4,512,128]{2,1,0:T(8,128)(2,1)}), bf16[4,512,128]{2,1,0:T(8,128)(2,1)S(1)}, u32[]{:S(2)}, u32[]{:S(2)}) async-start(bf16[4,512,128]{2,1,0:T(8,128)(2,1)} %stack.15), calls=%async_computation.6 | async-start | bytes 1048576 | tf_op jit(solution)/shard_map/all_to_all | solution.py:78
  218.7 12.9 %all-to-all-start.18 = ((bf16[4,512,128]{2,1,0:T(8,128)(2,1)}), bf16[4,512,128]{2,1,0:T(8,128)(2,1)S(1)}, u32[]{:S(2)}, u32[]{:S(2)}) async-start(bf16[4,512,128]{2,1,0:T(8,128)(2,1)} %broadcast_in_dim.20), calls=%async_computation.18 | async-start | bytes 1048576 | tf_op jit(solution)/shard_map/all_to_all | solution.py:23
  231.6 11.8 %all-to-all-start.7 = ((bf16[4,512,128]{1,2,0:T(8,128)(2,1)}), bf16[4,512,128]{1,2,0:T(8,128)(2,1)S(1)}, u32[]{:S(2)}, u32[]{:S(2)}) async-start(bf16[4,512,128]{1,2,0:T(8,128)(2,1)} %bitcast.147), calls=%async_computation.7 | async-start | bytes 1048576 | tf_op jit(solution)/shard_map/all_to_all | solution.py:17
  243.4 14.6 %all-to-all-start.19 = ((bf16[4,512,128]{1,2,0:T(8,128)(2,1)}), bf16[4,512,128]{1,2,0:T(8,128)(2,1)S(1)}, u32[]{:S(2)}, u32[]{:S(2)}) async-start(bf16[4,512,128]{1,2,0:T(8,128)(2,1)} %bitcast.141), calls=%async_computation.19 | async-start | bytes 1048576 | tf_op jit(solution)/shard_map/all_to_all | solution.py:17
  258.9 16.6 %all-to-all-start.8 = ((bf16[4,512,128]{2,1,0:T(8,128)(2,1)}), bf16[4,512,128]{2,1,0:T(8,128)(2,1)S(1)}, u32[]{:S(2)}, u32[]{:S(2)}) async-start(bf16[4,512,128]{2,1,0:T(8,128)(2,1)} %stack.16), calls=%async_computation.8 | async-start | bytes 1048576 | tf_op jit(solution)/shard_map/all_to_all | solution.py:78
  276.3 12.9 %all-to-all-start.20 = ((bf16[4,512,128]{2,1,0:T(8,128)(2,1)}), bf16[4,512,128]{2,1,0:T(8,128)(2,1)S(1)}, u32[]{:S(2)}, u32[]{:S(2)}) async-start(bf16[4,512,128]{2,1,0:T(8,128)(2,1)} %broadcast_in_dim.21), calls=%async_computation.20 | async-start | bytes 1048576 | tf_op jit(solution)/shard_map/all_to_all | solution.py:23
  289.2 11.8 %all-to-all-start.9 = ((bf16[4,512,128]{1,2,0:T(8,128)(2,1)}), bf16[4,512,128]{1,2,0:T(8,128)(2,1)S(1)}, u32[]{:S(2)}, u32[]{:S(2)}) async-start(bf16[4,512,128]{1,2,0:T(8,128)(2,1)} %bitcast.146), calls=%async_computation.9 | async-start | bytes 1048576 | tf_op jit(solution)/shard_map/all_to_all | solution.py:17
  301.0 14.6 %all-to-all-start.21 = ((bf16[4,512,128]{1,2,0:T(8,128)(2,1)}), bf16[4,512,128]{1,2,0:T(8,128)(2,1)S(1)}, u32[]{:S(2)}, u32[]{:S(2)}) async-start(bf16[4,512,128]{1,2,0:T(8,128)(2,1)} %bitcast.140), calls=%async_computation.21 | async-start | bytes 1048576 | tf_op jit(solution)/shard_map/all_to_all | solution.py:17
  316.5 16.6 %all-to-all-start.10 = ((bf16[4,512,128]{2,1,0:T(8,128)(2,1)}), bf16[4,512,128]{2,1,0:T(8,128)(2,1)S(1)}, u32[]{:S(2)}, u32[]{:S(2)}) async-start(bf16[4,512,128]{2,1,0:T(8,128)(2,1)} %stack.17), calls=%async_computation.10 | async-start | bytes 1048576 | tf_op jit(solution)/shard_map/all_to_all | solution.py:78
  334.0 12.9 %all-to-all-start.22 = ((bf16[4,512,128]{2,1,0:T(8,128)(2,1)}), bf16[4,512,128]{2,1,0:T(8,128)(2,1)S(1)}, u32[]{:S(2)}, u32[]{:S(2)}) async-start(bf16[4,512,128]{2,1,0:T(8,128)(2,1)} %broadcast_in_dim.22), calls=%async_computation.22 | async-start | bytes 1048576 | tf_op jit(solution)/shard_map/all_to_all | solution.py:23
  346.9 11.8 %all-to-all-start.11 = ((bf16[4,512,128]{1,2,0:T(8,128)(2,1)}), bf16[4,512,128]{1,2,0:T(8,128)(2,1)S(1)}, u32[]{:S(2)}, u32[]{:S(2)}) async-start(bf16[4,512,128]{1,2,0:T(8,128)(2,1)} %bitcast.145), calls=%async_computation.11 | async-start | bytes 1048576 | tf_op jit(solution)/shard_map/all_to_all | solution.py:17
  358.6 14.0 %all-to-all-start.23 = ((bf16[4,512,128]{1,2,0:T(8,128)(2,1)}), bf16[4,512,128]{1,2,0:T(8,128)(2,1)S(1)}, u32[]{:S(2)}, u32[]{:S(2)}) async-start(bf16[4,512,128]{1,2,0:T(8,128)(2,1)} %bitcast.139), calls=%async_computation.23 | async-start | bytes 1048576 | tf_op jit(solution)/shard_map/all_to_all | solution.py:17
  (11 other events, 137.8 us)
